TPU v7x, 32 devices: a whole 2x2x4 slice. The times are simulated.
32 devices in a mesh: phase: 16 (over z, y, x), lat: 2 (over core).
Axes of the slice: x: 2, y: 2, z: 4, core: 2. Of those that a mesh axis runs over, the one named last changes fastest.
Arguments:
- state_now: float32 [3, 64, 1024], P(None, ('lat', 'phase')), may hold values from -4 to 4
- ocean_depth: float32 [64, 1024], P('lat'), may hold values from 0.5 to 1.5
- coriolis: float32 [64], P('lat'), may hold values from -0.4 to 0.4
- phase_times: float32 [16], P('phase'), may hold values from -6 to 6
- phase_weights: float32 [16], P('phase'), may hold values from 0.00625 to 0.25
Outputs:
- state_next: float32 [3, 64, 1024], P(None, ('lat', 'phase'))
- tendency: float32 [3, 64, 1024], P(None, ('lat', 'phase'))
All inputs are finite; a program needn't handle non-finite values.
Results may differ from a plain program's by a relative error of at most 0.00002.
Values sent between devices are 32-bit elements; how exact they have to be, the bound alone decides.
A program may use at most 64 MiB of HBM per device.

v0:
```python
import math
import jax
import jax.numpy as jnp
from jax import lax
from jax.sharding import PartitionSpec as P

DEG = 8
DEPTH = 4
radius_scale = 2.5
time_step = 0.5
series_terms = 20


def extended(shard, sides, width):
    for axis, dim in sides:
        devices, length = (lax.axis_size(axis), shard.shape[dim])
        up = [(i, (i + 1) % devices) for i in range(devices - 1)]
        down = [(j, i) for i, j in up]
        last = lax.slice_in_dim(shard, length - width, length, axis=dim)
        first = lax.slice_in_dim(shard, 0, width, axis=dim)
        before = lax.ppermute(last, axis, up)
        after = lax.ppermute(first, axis, down)
        shard = jnp.concatenate([before, shard, after], axis=dim)
    return shard


def along_lon(values):
    return (jnp.roll(values, -1, axis=-1) - jnp.roll(values, 1, axis=-1)) * 0.5


def along_lat(values):
    return (values[..., 2:, :] - values[..., :-2, :]) * 0.5


def interior(values):
    return values[..., 1:-1, :]


def wave_operator(fields, coefficients):
    height = fields[:, 0]
    eastward = fields[:, 1]
    northward = fields[:, 2]
    depth_field = coefficients[0]
    rotation = coefficients[1]
    out_height = -(along_lon(interior(depth_field * eastward)) + along_lat(depth_field * northward))
    out_east = -along_lon(interior(height)) + interior(rotation * northward)
    out_north = -along_lat(height) - interior(rotation * eastward)
    return jnp.stack([out_height, out_east, out_north], axis=1) / radius_scale


def advection(fields):
    height = fields[:, 0]
    eastward = fields[:, 1]
    northward = fields[:, 2]
    mid_east = interior(eastward)
    mid_north = interior(northward)
    out_height = -(along_lon(interior(height * eastward)) + along_lat(height * northward))
    out_east = -(mid_east * along_lon(mid_east) + mid_north * along_lat(eastward))
    out_north = -(mid_east * along_lon(mid_north) + mid_north * along_lat(northward))
    return jnp.stack([out_height, out_east, out_north], axis=1)


def series_coeffs(sample_time):
    half_time = sample_time * 0.5
    square = half_time * half_time
    result = []
    for degree in range(DEG + 1):
        summed = jnp.zeros_like(sample_time)
        term_sq = jnp.ones_like(sample_time)
        for series in range(series_terms):
            factor = (-1.0) ** series / (math.factorial(series) * math.factorial(series + degree))
            summed = summed + factor * term_sq
            term_sq = term_sq * square
        result.append(summed * half_time**degree)
    return result


def trimmed(values, have, wanted):
    excess = have - wanted
    if excess == 0:
        return values
    return values[:, :, excess : values.shape[2] - excess]


def per_device(state_now, ocean_depth, coriolis, phase_times, phase_weights):
    tile_rows = ocean_depth.shape[0]
    lat_count = lax.axis_size("lat")
    lat_place = lax.axis_index("lat")
    stacked = jnp.stack([ocean_depth, jnp.broadcast_to(coriolis[:, None], ocean_depth.shape)])
    coefficients = extended(stacked, (("lat", 1),), DEPTH)
    global_rows = lat_place * tile_rows - DEPTH + jnp.arange(tile_rows + 2 * DEPTH, dtype=jnp.int32)
    inside = ((global_rows >= 0) & (global_rows < tile_rows * lat_count)).astype(jnp.float32)
    forward = series_coeffs(phase_times)
    backward = series_coeffs(-phase_times)
    sample_count = phase_times.shape[0]

    def band_coeffs(margin):
        return coefficients[:, DEPTH - margin : DEPTH + tile_rows + margin]

    def band_inside(margin):
        return inside[DEPTH - margin : DEPTH + tile_rows + margin][None, None, :, None]

    def exponential(fields, series):
        accumulated = series[0][:, None, None, None] * fields
        previous = None
        current = fields
        width_prev = 0
        width_cur = 0
        for degree in range(1, DEG + 1):
            if (degree - 1) % DEPTH == 0:
                if previous is None:
                    current = extended(current, (("lat", 2),), DEPTH)
                else:
                    joined = jnp.concatenate(
                        [trimmed(previous, width_prev, 0), trimmed(current, width_cur, 0)], axis=0
                    )
                    joined = extended(joined, (("lat", 2),), DEPTH)
                    previous = joined[:sample_count]
                    current = joined[sample_count:]
                    width_prev = DEPTH
                width_cur = DEPTH
            width_new = width_cur - 1
            applied = wave_operator(current, band_coeffs(width_cur))
            if previous is None:
                advanced = applied
            else:
                advanced = 2.0 * applied + trimmed(previous, width_prev, width_new)
            advanced = advanced * band_inside(width_new)
            accumulated = accumulated + 2.0 * series[degree][:, None, None, None] * trimmed(
                advanced, width_new, 0
            )
            previous = current
            width_prev = width_cur
            current = advanced
            width_cur = width_new
        return accumulated

    def averaged(whole_tile):
        samples = whole_tile[None]
        waves = exponential(samples, forward)
        rimmed = extended(waves, (("lat", 2),), 1)
        pulled = advection(rimmed)
        returned = exponential(pulled, backward)
        return jnp.sum(phase_weights[:, None, None, None] * returned, axis=0)

    whole_tile = lax.all_gather(state_now, "phase", axis=1, tiled=True)

    def summed_whole(partial_value):
        return lax.psum(partial_value, "phase")

    first = summed_whole(averaged(whole_tile))
    middle = whole_tile + time_step * first
    second = summed_whole(averaged(middle))
    tendency_tile = 0.5 * (first + second)
    share = state_now.shape[1]
    start = lax.axis_index("phase") * share
    tendency = lax.dynamic_slice_in_dim(tendency_tile, start, share, 1)
    state_next = state_now + time_step * tendency
    return (state_next, tendency)


def solution(mesh):
    placed = (P(None, ("lat", "phase"), None), P("lat", None), P("lat"), P("phase"), P("phase"))
    return jax.shard_map(
        per_device,
        mesh=mesh,
        in_specs=placed,
        out_specs=(P(None, ("lat", "phase"), None), P(None, ("lat", "phase"), None)),
        check_vma=False,
    )
```

profile of v0, /device:TPU:0, one launch (start us, length us, event | category | flops | bytes accessed | tf_op | source)
XLA Modules:
  0.0 368.3 jit_solution(13352655160559666389)
XLA Ops:
  8.0 45.3 %all_gather.3 = f32[3,32,1024]{2,0,1:T(4,128)S(1)} all-gather(f32[3,2,1024]{2,0,1:T(4,128)S(1)} %copy.168), channel_id=1, replica_groups=mesh['phase'=16,'lat'=2] {'phase'}, dimensions={1}, use_global_device_ids=true | all-gather | bytes 417792 | tf_op jit(solution)/shard_map/all_gather | solution.py:146
  53.6 1.4 collective-permute-start.3
  55.0 3.0 collective-permute-start.2
  58.2 1.3 collective-permute-start.1
  59.5 3.0 collective-permute-start
  67.0 1.3 collective-permute-start.5
  68.3 3.0 collective-permute-start.4
  76.5 1.3 collective-permute-start.7
  77.8 3.0 collective-permute-start.6
  82.7 1.3 collective-permute-start.9
  84.0 3.0 collective-permute-start.8
  91.5 1.3 collective-permute-start.11
  92.8 3.2 collective-permute-start.10
  100.2 1.3 fusion.41
  101.6 104.9 %all-reduce.3.cloned.1.call-done = f32[3,32,1024]{2,1,0:T(8,128)} async-done(((f32[3,32,1024]{2,1,0:T(8,128)}), f32[3,32,1024]{2,1,0:T(8,128)}) %all-reduce.3.cloned.1.call-update) | async-done | bytes 393232 | tf_op jit(solution)/shard_map/psum | solution.py:149
  206.5 1.2 fusion.500
  207.8 1.3 collective-permute-start.13
  209.1 3.0 collective-permute-start.12
  216.6 1.3 collective-permute-start.15
  217.9 3.0 collective-permute-start.14
  220.9 0.9 collective-permute-done.14
  225.4 0.9 copy-done
  227.0 1.3 collective-permute-start.17
  228.3 3.0 collective-permute-start.16
  233.2 1.3 collective-permute-start.19
  234.5 3.3 collective-permute-start.18
  241.9 1.3 collective-permute-start.21
  243.2 3.0 collective-permute-start.20
  246.3 0.9 collective-permute-done.20
  250.7 1.3 fusion.23
  252.0 107.9 %all-reduce.5.cloned.1.call-done = f32[3,32,1024]{2,1,0:T(8,128)} async-done(((f32[3,32,1024]{2,1,0:T(8,128)}), f32[3,32,1024]{2,1,0:T(8,128)}) %all-reduce.5.cloned.1.call-update) | async-done | bytes 393232 | tf_op jit(solution)/shard_map/psum | solution.py:149
  359.9 1.5 multiply_add_fusion.1
  (372 shorter events, 36.3 us)
Async XLA Ops:
  7.2 199.3 %all-reduce.3.cloned.1.call-start = ((), (), s32[]{:S(2)}) async-start(), calls=%async_computation | async-start | bytes 786432 | tf_op jit(solution)/shard_map/psum | solution.py:149
  53.5 4.6 %copy-start.1 = (f32[32,1024]{1,0:T(8,128)S(1)}, f32[32,1024]{1,0:T(8,128)}, u32[]{:S(2)}) copy-start(f32[32,1024]{1,0:T(8,128)} %param.6) | copy-start | bytes 393220
  53.6 4.5 %copy-start.3 = (f32[32]{0:T(128)S(1)}, f32[32]{0:T(128)}, u32[]{:S(2)}) copy-start(f32[32]{0:T(128)} %param.7) | copy-start | bytes 388
  53.6 9.8 %collective-permute-start.3 = (f32[1,3,4,1024]{3,2,1,0:T(4,128)S(1)}, f32[1,3,4,1024]{3,2,1,0:T(4,128)S(1)}, u32[]{:S(2)}, u32[]{:S(2)}) collective-permute-start(f32[1,3,4,1024]{3,2,1,0:T(4,128)S(1)} %get-tuple-element.195), channel_id=1, source_target_pairs={{1,0},{3,2},{5,4},{7,6},{9,8},{11,10},{13,12},{15,14},{17,16},{19,... | collective-permute-start | bytes 147464 | tf_op jit(solution)/shard_map/ppermute | solution.py:22
  55.0 8.4 %collective-permute-start.2 = (f32[1,3,4,1024]{3,2,1,0:T(4,128)S(1)}, f32[1,3,4,1024]{3,2,1,0:T(4,128)S(1)}, u32[]{:S(2)}, u32[]{:S(2)}) collective-permute-start(f32[1,3,4,1024]{3,2,1,0:T(4,128)S(1)} %get-tuple-element.194), channel_id=1, source_target_pairs={{0,1},{2,3},{4,5},{6,7},{8,9},{10,11},{12,13},{14,15},{16,17},{18,... | collective-permute-start | bytes 147464 | tf_op jit(solution)/shard_map/ppermute | solution.py:21
  58.2 4.6 %collective-permute-start.1 = (f32[2,4,1024]{2,1,0:T(4,128)S(1)}, f32[2,4,1024]{2,1,0:T(4,128)S(1)}, u32[]{:S(2)}, u32[]{:S(2)}) collective-permute-start(f32[2,4,1024]{2,1,0:T(4,128)S(1)} %get-tuple-element.205), channel_id=1, source_target_pairs={{1,0},{3,2},{5,4},{7,6},{9,8},{11,10},{13,12},{15,14},{17,16},{19,... | collective-permute-start | bytes 98312 | tf_op jit(solution)/shard_map/ppermute | solution.py:22
  59.5 3.9 %collective-permute-start = (f32[2,4,1024]{2,1,0:T(4,128)S(1)}, f32[2,4,1024]{2,1,0:T(4,128)S(1)}, u32[]{:S(2)}, u32[]{:S(2)}) collective-permute-start(f32[2,4,1024]{2,1,0:T(4,128)S(1)} %get-tuple-element.204), channel_id=1, source_target_pairs={{0,1},{2,3},{4,5},{6,7},{8,9},{10,11},{12,13},{14,15},{16,17},{18,... | collective-permute-start | bytes 98312 | tf_op jit(solution)/shard_map/ppermute | solution.py:21
  67.0 5.3 %collective-permute-start.5 = (f32[2,3,4,1024]{3,2,1,0:T(4,128)S(1)}, f32[2,3,4,1024]{3,2,1,0:T(4,128)S(1)}, u32[]{:S(2)}, u32[]{:S(2)}) collective-permute-start(f32[2,3,4,1024]{3,2,1,0:T(4,128)S(1)} %get-tuple-element.91), channel_id=1, source_target_pairs={{1,0},{3,2},{5,4},{7,6},{9,8},{11,10},{13,12},{15,14},{17,16},{19,... | collective-permute-start | bytes 294920 | tf_op jit(solution)/shard_map/ppermute | solution.py:22
  68.3 4.0 %collective-permute-start.4 = (f32[2,3,4,1024]{3,2,1,0:T(4,128)S(1)}, f32[2,3,4,1024]{3,2,1,0:T(4,128)S(1)}, u32[]{:S(2)}, u32[]{:S(2)}) collective-permute-start(f32[2,3,4,1024]{3,2,1,0:T(4,128)S(1)} %get-tuple-element.90), channel_id=1, source_target_pairs={{0,1},{2,3},{4,5},{6,7},{8,9},{10,11},{12,13},{14,15},{16,17},{18,... | collective-permute-start | bytes 294920 | tf_op jit(solution)/shard_map/ppermute | solution.py:21
  76.5 4.3 %collective-permute-start.7 = (f32[1,3,1,1024]{3,2,1,0:T(1,128)S(1)}, f32[1,3,1,1024]{3,2,1,0:T(1,128)S(1)}, u32[]{:S(2)}, u32[]{:S(2)}) collective-permute-start(f32[1,3,1,1024]{3,2,1,0:T(1,128)S(1)} %get-tuple-element.193), channel_id=1, source_target_pairs={{1,0},{3,2},{5,4},{7,6},{9,8},{11,10},{13,12},{15,14},{17,16},{19,... | collective-permute-start | bytes 36872 | tf_op jit(solution)/shard_map/ppermute | solution.py:22
  77.8 3.9 %collective-permute-start.6 = (f32[1,3,1,1024]{3,2,1,0:T(1,128)S(1)}, f32[1,3,1,1024]{3,2,1,0:T(1,128)S(1)}, u32[]{:S(2)}, u32[]{:S(2)}) collective-permute-start(f32[1,3,1,1024]{3,2,1,0:T(1,128)S(1)} %get-tuple-element.192), channel_id=1, source_target_pairs={{0,1},{2,3},{4,5},{6,7},{8,9},{10,11},{12,13},{14,15},{16,17},{18,... | collective-permute-start | bytes 36872 | tf_op jit(solution)/shard_map/ppermute | solution.py:21
  82.7 4.3 %collective-permute-start.9 = (f32[1,3,4,1024]{3,2,1,0:T(4,128)S(1)}, f32[1,3,4,1024]{3,2,1,0:T(4,128)S(1)}, u32[]{:S(2)}, u32[]{:S(2)}) collective-permute-start(f32[1,3,4,1024]{3,2,1,0:T(4,128)S(1)} %get-tuple-element.191), channel_id=1, source_target_pairs={{1,0},{3,2},{5,4},{7,6},{9,8},{11,10},{13,12},{15,14},{17,16},{19,... | collective-permute-start | bytes 147464 | tf_op jit(solution)/shard_map/ppermute | solution.py:22
  84.0 3.9 %collective-permute-start.8 = (f32[1,3,4,1024]{3,2,1,0:T(4,128)S(1)}, f32[1,3,4,1024]{3,2,1,0:T(4,128)S(1)}, u32[]{:S(2)}, u32[]{:S(2)}) collective-permute-start(f32[1,3,4,1024]{3,2,1,0:T(4,128)S(1)} %get-tuple-element.190), channel_id=1, source_target_pairs={{0,1},{2,3},{4,5},{6,7},{8,9},{10,11},{12,13},{14,15},{16,17},{18,... | collective-permute-start | bytes 147464 | tf_op jit(solution)/shard_map/ppermute | solution.py:21
  91.5 5.2 %collective-permute-start.11 = (f32[2,3,4,1024]{3,2,1,0:T(4,128)S(1)}, f32[2,3,4,1024]{3,2,1,0:T(4,128)S(1)}, u32[]{:S(2)}, u32[]{:S(2)}) collective-permute-start(f32[2,3,4,1024]{3,2,1,0:T(4,128)S(1)} %get-tuple-element.89), channel_id=1, source_target_pairs={{1,0},{3,2},{5,4},{7,6},{9,8},{11,10},{13,12},{15,14},{17,16},{19,... | collective-permute-start | bytes 294920 | tf_op jit(solution)/shard_map/ppermute | solution.py:22
  92.8 4.0 %collective-permute-start.10 = (f32[2,3,4,1024]{3,2,1,0:T(4,128)S(1)}, f32[2,3,4,1024]{3,2,1,0:T(4,128)S(1)}, u32[]{:S(2)}, u32[]{:S(2)}) collective-permute-start(f32[2,3,4,1024]{3,2,1,0:T(4,128)S(1)} %get-tuple-element.88), channel_id=1, source_target_pairs={{0,1},{2,3},{4,5},{6,7},{8,9},{10,11},{12,13},{14,15},{16,17},{18,... | collective-permute-start | bytes 294920 | tf_op jit(solution)/shard_map/ppermute | solution.py:21
  101.6 258.3 %all-reduce.5.cloned.1.call-start = ((), (), s32[]{:S(2)}) async-start(), calls=%async_computation.1 | async-start | bytes 786432 | tf_op jit(solution)/shard_map/psum | solution.py:149
  207.8 4.3 %collective-permute-start.13 = (f32[1,3,4,1024]{3,2,1,0:T(4,128)S(1)}, f32[1,3,4,1024]{3,2,1,0:T(4,128)S(1)}, u32[]{:S(2)}, u32[]{:S(2)}) collective-permute-start(f32[1,3,4,1024]{3,2,1,0:T(4,128)S(1)} %get-tuple-element.189), channel_id=1, source_target_pairs={{1,0},{3,2},{5,4},{7,6},{9,8},{11,10},{13,12},{15,14},{17,16},{19,... | collective-permute-start | bytes 147464 | tf_op jit(solution)/shard_map/ppermute | solution.py:22
  209.1 3.9 %collective-permute-start.12 = (f32[1,3,4,1024]{3,2,1,0:T(4,128)S(1)}, f32[1,3,4,1024]{3,2,1,0:T(4,128)S(1)}, u32[]{:S(2)}, u32[]{:S(2)}) collective-permute-start(f32[1,3,4,1024]{3,2,1,0:T(4,128)S(1)} %get-tuple-element.188), channel_id=1, source_target_pairs={{0,1},{2,3},{4,5},{6,7},{8,9},{10,11},{12,13},{14,15},{16,17},{18,... | collective-permute-start | bytes 147464 | tf_op jit(solution)/shard_map/ppermute | solution.py:21
  216.6 4.3 %collective-permute-start.15 = (f32[2,3,4,1024]{3,2,1,0:T(4,128)S(1)}, f32[2,3,4,1024]{3,2,1,0:T(4,128)S(1)}, u32[]{:S(2)}, u32[]{:S(2)}) collective-permute-start(f32[2,3,4,1024]{3,2,1,0:T(4,128)S(1)} %get-tuple-element.87), channel_id=1, source_target_pairs={{1,0},{3,2},{5,4},{7,6},{9,8},{11,10},{13,12},{15,14},{17,16},{19,... | collective-permute-start | bytes 294920 | tf_op jit(solution)/shard_map/ppermute | solution.py:22
  217.9 4.0 %collective-permute-start.14 = (f32[2,3,4,1024]{3,2,1,0:T(4,128)S(1)}, f32[2,3,4,1024]{3,2,1,0:T(4,128)S(1)}, u32[]{:S(2)}, u32[]{:S(2)}) collective-permute-start(f32[2,3,4,1024]{3,2,1,0:T(4,128)S(1)} %get-tuple-element.86), channel_id=1, source_target_pairs={{0,1},{2,3},{4,5},{6,7},{8,9},{10,11},{12,13},{14,15},{16,17},{18,... | collective-permute-start | bytes 294920 | tf_op jit(solution)/shard_map/ppermute | solution.py:21
  225.2 1.0 copy-start
  227.0 4.3 %collective-permute-start.17 = (f32[1,3,1,1024]{3,2,1,0:T(1,128)S(1)}, f32[1,3,1,1024]{3,2,1,0:T(1,128)S(1)}, u32[]{:S(2)}, u32[]{:S(2)}) collective-permute-start(f32[1,3,1,1024]{3,2,1,0:T(1,128)S(1)} %get-tuple-element.187), channel_id=1, source_target_pairs={{1,0},{3,2},{5,4},{7,6},{9,8},{11,10},{13,12},{15,14},{17,16},{19,... | collective-permute-start | bytes 36872 | tf_op jit(solution)/shard_map/ppermute | solution.py:22
  228.3 3.9 %collective-permute-start.16 = (f32[1,3,1,1024]{3,2,1,0:T(1,128)S(1)}, f32[1,3,1,1024]{3,2,1,0:T(1,128)S(1)}, u32[]{:S(2)}, u32[]{:S(2)}) collective-permute-start(f32[1,3,1,1024]{3,2,1,0:T(1,128)S(1)} %get-tuple-element.186), channel_id=1, source_target_pairs={{0,1},{2,3},{4,5},{6,7},{8,9},{10,11},{12,13},{14,15},{16,17},{18,... | collective-permute-start | bytes 36872 | tf_op jit(solution)/shard_map/ppermute | solution.py:21
  233.2 4.6 %collective-permute-start.19 = (f32[1,3,4,1024]{3,2,1,0:T(4,128)S(1)}, f32[1,3,4,1024]{3,2,1,0:T(4,128)S(1)}, u32[]{:S(2)}, u32[]{:S(2)}) collective-permute-start(f32[1,3,4,1024]{3,2,1,0:T(4,128)S(1)} %get-tuple-element.185), channel_id=1, source_target_pairs={{1,0},{3,2},{5,4},{7,6},{9,8},{11,10},{13,12},{15,14},{17,16},{19,... | collective-permute-start | bytes 147464 | tf_op jit(solution)/shard_map/ppermute | solution.py:22
  234.5 3.9 %collective-permute-start.18 = (f32[1,3,4,1024]{3,2,1,0:T(4,128)S(1)}, f32[1,3,4,1024]{3,2,1,0:T(4,128)S(1)}, u32[]{:S(2)}, u32[]{:S(2)}) collective-permute-start(f32[1,3,4,1024]{3,2,1,0:T(4,128)S(1)} %get-tuple-element.184), channel_id=1, source_target_pairs={{0,1},{2,3},{4,5},{6,7},{8,9},{10,11},{12,13},{14,15},{16,17},{18,... | collective-permute-start | bytes 147464 | tf_op jit(solution)/shard_map/ppermute | solution.py:21
  241.9 4.3 %collective-permute-start.21 = (f32[2,3,4,1024]{3,2,1,0:T(4,128)S(1)}, f32[2,3,4,1024]{3,2,1,0:T(4,128)S(1)}, u32[]{:S(2)}, u32[]{:S(2)}) collective-permute-start(f32[2,3,4,1024]{3,2,1,0:T(4,128)S(1)} %get-tuple-element.85), channel_id=1, source_target_pairs={{1,0},{3,2},{5,4},{7,6},{9,8},{11,10},{13,12},{15,14},{17,16},{19,... | collective-permute-start | bytes 294920 | tf_op jit(solution)/shard_map/ppermute | solution.py:22
  243.2 4.0 %collective-permute-start.20 = (f32[2,3,4,1024]{3,2,1,0:T(4,128)S(1)}, f32[2,3,4,1024]{3,2,1,0:T(4,128)S(1)}, u32[]{:S(2)}, u32[]{:S(2)}) collective-permute-start(f32[2,3,4,1024]{3,2,1,0:T(4,128)S(1)} %get-tuple-element.84), channel_id=1, source_target_pairs={{0,1},{2,3},{4,5},{6,7},{8,9},{10,11},{12,13},{14,15},{16,17},{18,... | collective-permute-start | bytes 294920 | tf_op jit(solution)/shard_map/ppermute | solution.py:21
  252.0 107.9 %copy-start.2 = (f32[3,2,1024]{2,1,0:T(2,128)S(1)}, f32[3,2,1024]{2,1,0:T(2,128)}, u32[]{:S(2)}) copy-start(f32[3,2,1024]{2,1,0:T(2,128)} %param.5) | copy-start | bytes 73732
Sparse Core Ops, SparseCore 0:
  101.7 104.7 all-reduce.2
  252.1 107.7 all-reduce.4
where the time goes:
time: 369 us; the launch traced here: 368 us
  waiting for transfers between devices  219 us (59%)
  starting transfers between devices  48.2 us (13%)
  blocking collectives  45.3 us (12%)
  other arithmetic  21.8 us (6%)
  between operations  17.7 us (5%)
  local copies, waits for them, and re-layouts  16.1 us (4%)
    psum x2, waiting for transfers between devices, summed_whole(): return lax.psum(partial_value, 'phase')  213 us
    all_gather x1, blocking collectives, per_device(): whole_tile = lax.all_gather(state_now, 'phase', axis=1, tiled=True)  45.3 us
    ppermute x11, starting transfers between devices, extended(): before = lax.ppermute(last, axis, up)  33.8 us
    ppermute x11, starting transfers between devices, extended(): after = lax.ppermute(first, axis, down)  14.3 us
    slice x140, local copies, waits for them, and re-layouts, along_lon(): return (jnp.roll(values, -1, axis=-1) - jnp.roll(values, 1, axis=-1)) * 0.5  12.7 us
    another operation x63, other arithmetic, wave_operator(): return jnp.stack([out_height, out_east, out_north], axis=1) / radius_scale  7.91 us
  transfers between devices with their start and end apart: 24, of which 10 were waited for; matrix products, arithmetic and copies ran while one was open for 0% of the time, Pallas kernels for 0%

commit v1 on v0

--- a/solution.py
+++ b/solution.py
@@ -146,7 +146,7 @@
     whole_tile = lax.all_gather(state_now, "phase", axis=1, tiled=True)
 
     def summed_whole(partial_value):
-        return lax.psum(partial_value, "phase")
+        return jnp.sum(lax.all_gather(partial_value, "phase"), axis=0)
 
     first = summed_whole(averaged(whole_tile))
     middle = whole_tile + time_step * first

time: 369 us -> 341 us (0.924)
  waiting for transfers between devices: 219 us -> 197 us
  starting transfers between devices: 48.2 us -> 36.7 us
  other arithmetic: 21.8 us -> 28.2 us
    psum x2 -> x0, waiting for transfers between devices: 213 us -> none  [summed_whole(): return lax.psum(partial_value, 'phase')]
    all_gather x0 -> x2, waiting for transfers between devices: none -> 182 us  [summed_whole(): return jnp.sum(lax.all_gather(partial_value, 'phase'), axis=0)]
    ppermute x11, waiting for transfers between devices: 0.03 us -> 15 us  [extended(): after = lax.ppermute(first, axis, down)]
    ppermute x11, starting transfers between devices: 33.8 us -> 22 us  [extended(): before = lax.ppermute(last, axis, up)]
    ppermute x11, waiting for transfers between devices: 6.34 us -> 0.03 us  [extended(): before = lax.ppermute(last, axis, up)]
    reduce_sum x2, other arithmetic: 2.59 us -> 6.71 us  [summed_whole(): return jnp.sum(lax.all_gather(partial_value, 'phase'), axis=0)]
  transfers between devices with their start and end apart: 24 -> 24, of which waited for: 10 -> 12; matrix products, arithmetic and copies ran while one was open for 0% -> 1% of each run, Pallas kernels for 0% -> 0%
where the time goes in v1:
time: 341 us; the launch traced here: 340 us
  waiting for transfers between devices  197 us (58%)
  blocking collectives  44.9 us (13%)
  starting transfers between devices  36.7 us (11%)
  other arithmetic  28.2 us (8%)
  between operations  17.7 us (5%)
  local copies, waits for them, and re-layouts  15.9 us (5%)
    all_gather x2, waiting for transfers between devices, summed_whole(): return jnp.sum(lax.all_gather(partial_value, 'phase'), axis=0)  182 us
    all_gather x1, blocking collectives, per_device(): whole_tile = lax.all_gather(state_now, 'phase', axis=1, tiled=True)  44.9 us
    ppermute x11, starting transfers between devices, extended(): before = lax.ppermute(last, axis, up)  22 us
    ppermute x11, waiting for transfers between devices, extended(): after = lax.ppermute(first, axis, down)  15 us
    ppermute x11, starting transfers between devices, extended(): after = lax.ppermute(first, axis, down)  14.6 us
    slice x140, local copies, waits for them, and re-layouts, along_lon(): return (jnp.roll(values, -1, axis=-1) - jnp.roll(values, 1, axis=-1)) * 0.5  12.7 us
    another operation x63, other arithmetic, wave_operator(): return jnp.stack([out_height, out_east, out_north], axis=1) / radius_scale  7.87 us
  transfers between devices with their start and end apart: 24, of which 12 were waited for; matrix products, arithmetic and copies ran while one was open for 1% of the time, Pallas kernels for 0%

profile of v1, /device:TPU:0, one launch (start us, length us, event | category | flops | bytes accessed | tf_op | source)
XLA Modules:
  0.0 340.4 jit_solution(13037211647707222856)
XLA Ops:
  8.7 2.4 collective-permute-start
  11.1 1.3 collective-permute-start.1
  13.2 44.9 %all_gather.11 = f32[3,32,1024]{2,0,1:T(4,128)S(1)} all-gather(f32[3,2,1024]{2,0,1:T(4,128)S(1)} %copy.248), channel_id=1, replica_groups=mesh['phase'=16,'lat'=2] {'phase'}, dimensions={1}, use_global_device_ids=true | all-gather | bytes 417792 | tf_op jit(solution)/shard_map/all_gather | solution.py:146
  58.4 1.3 collective-permute-start.2
  59.7 1.3 collective-permute-start.3
  66.4 2.5 collective-permute-start.4
  68.9 1.3 collective-permute-start.5
  76.3 2.1 collective-permute-start.6
  78.4 1.3 collective-permute-start.7
  79.8 1.8 collective-permute-done.7
  82.5 2.1 collective-permute-start.8
  84.6 1.3 collective-permute-start.9
  85.9 1.8 collective-permute-done.9
  91.3 2.1 collective-permute-start.10
  93.4 1.5 collective-permute-start.11
  100.1 1.3 fusion.39
  101.5 89.4 %all-gather.3.cloned.1.call-done = f32[16,3,32,1024]{3,2,1,0:T(8,128)} async-done(((f32[1,3,32,1024]{3,2,1,0:T(8,128)}), f32[16,3,32,1024]{3,2,1,0:T(8,128)}) %all-gather.3.cloned.1.call-update) | async-done | bytes 6291472 | tf_op jit(solution)/shard_map/all_gather | solution.py:149
  190.9 3.4 reduce_sum.16
  197.1 1.8 collective-permute-done.13
  202.5 2.1 collective-permute-start.14
  205.9 1.9 collective-permute-done.15
  212.1 2.1 collective-permute-start.16
  214.1 1.3 collective-permute-start.17
  215.4 1.8 collective-permute-done.17
  218.2 2.1 collective-permute-start.18
  220.3 1.5 collective-permute-start.19
  221.8 1.6 collective-permute-done.19
  227.0 2.1 collective-permute-start.20
  230.4 1.9 collective-permute-done.21
  235.8 1.3 fusion.22
  237.1 92.4 %all-gather.5.cloned.1.call-done = f32[16,3,32,1024]{3,2,1,0:T(8,128)} async-done(((f32[1,3,32,1024]{3,2,1,0:T(8,128)}), f32[16,3,32,1024]{3,2,1,0:T(8,128)}) %all-gather.5.cloned.1.call-update) | async-done | bytes 6291472 | tf_op jit(solution)/shard_map/all_gather | solution.py:149
  329.5 3.4 reduce_sum.20
  (368 shorter events, 42.6 us)
Async XLA Ops:
  7.2 183.7 %all-gather.3.cloned.1.call-start = ((), (), s32[]{:S(2)}) async-start(), calls=%async_computation | async-start | bytes 6684672 | tf_op jit(solution)/shard_map/all_gather | solution.py:149
  8.7 52.6 %collective-permute-start = (f32[2,4,1024]{2,1,0:T(4,128)S(1)}, f32[2,4,1024]{2,1,0:T(4,128)S(1)}, u32[]{:S(2)}, u32[]{:S(2)}) collective-permute-start(f32[2,4,1024]{2,1,0:T(4,128)S(1)} %get-tuple-element.206), channel_id=1, source_target_pairs={{0,1},{2,3},{4,5},{6,7},{8,9},{10,11},{12,13},{14,15},{16,17},{18,... | collective-permute-start | bytes 98312 | tf_op jit(solution)/shard_map/ppermute | solution.py:21
  11.1 50.2 %collective-permute-start.1 = (f32[2,4,1024]{2,1,0:T(4,128)S(1)}, f32[2,4,1024]{2,1,0:T(4,128)S(1)}, u32[]{:S(2)}, u32[]{:S(2)}) collective-permute-start(f32[2,4,1024]{2,1,0:T(4,128)S(1)} %get-tuple-element.207), channel_id=1, source_target_pairs={{1,0},{3,2},{5,4},{7,6},{9,8},{11,10},{13,12},{15,14},{17,16},{19,... | collective-permute-start | bytes 98312 | tf_op jit(solution)/shard_map/ppermute | solution.py:22
  58.4 3.9 %collective-permute-start.2 = (f32[1,3,4,1024]{3,2,1,0:T(4,128)S(1)}, f32[1,3,4,1024]{3,2,1,0:T(4,128)S(1)}, u32[]{:S(2)}, u32[]{:S(2)}) collective-permute-start(f32[1,3,4,1024]{3,2,1,0:T(4,128)S(1)} %get-tuple-element.196), channel_id=1, source_target_pairs={{0,1},{2,3},{4,5},{6,7},{8,9},{10,11},{12,13},{14,15},{16,17},{18,... | collective-permute-start | bytes 147464 | tf_op jit(solution)/shard_map/ppermute | solution.py:21
  59.7 3.1 collective-permute-start.3
  66.4 4.8 %collective-permute-start.4 = (f32[2,3,4,1024]{3,2,1,0:T(4,128)S(1)}, f32[2,3,4,1024]{3,2,1,0:T(4,128)S(1)}, u32[]{:S(2)}, u32[]{:S(2)}) collective-permute-start(f32[2,3,4,1024]{3,2,1,0:T(4,128)S(1)} %get-tuple-element.92), channel_id=1, source_target_pairs={{0,1},{2,3},{4,5},{6,7},{8,9},{10,11},{12,13},{14,15},{16,17},{18,... | collective-permute-start | bytes 294920 | tf_op jit(solution)/shard_map/ppermute | solution.py:21
  68.9 3.2 collective-permute-start.5
  76.3 3.5 %collective-permute-start.6 = (f32[1,3,1,1024]{3,2,1,0:T(1,128)S(1)}, f32[1,3,1,1024]{3,2,1,0:T(1,128)S(1)}, u32[]{:S(2)}, u32[]{:S(2)}) collective-permute-start(f32[1,3,1,1024]{3,2,1,0:T(1,128)S(1)} %get-tuple-element.194), channel_id=1, source_target_pairs={{0,1},{2,3},{4,5},{6,7},{8,9},{10,11},{12,13},{14,15},{16,17},{18,... | collective-permute-start | bytes 36872 | tf_op jit(solution)/shard_map/ppermute | solution.py:21
  78.4 3.1 collective-permute-start.7
  82.5 3.4 collective-permute-start.8
  84.6 3.1 collective-permute-start.9
  91.3 4.2 %collective-permute-start.10 = (f32[2,3,4,1024]{3,2,1,0:T(4,128)S(1)}, f32[2,3,4,1024]{3,2,1,0:T(4,128)S(1)}, u32[]{:S(2)}, u32[]{:S(2)}) collective-permute-start(f32[2,3,4,1024]{3,2,1,0:T(4,128)S(1)} %get-tuple-element.90), channel_id=1, source_target_pairs={{0,1},{2,3},{4,5},{6,7},{8,9},{10,11},{12,13},{14,15},{16,17},{18,... | collective-permute-start | bytes 294920 | tf_op jit(solution)/shard_map/ppermute | solution.py:21
  93.4 3.2 collective-permute-start.11
  101.4 228.1 %all-gather.5.cloned.1.call-start = ((), (), s32[]{:S(2)}) async-start(), calls=%async_computation.1 | async-start | bytes 6684672 | tf_op jit(solution)/shard_map/all_gather | solution.py:149
  194.5 2.6 collective-permute-start.12
  195.8 3.1 collective-permute-start.13
  202.5 3.4 collective-permute-start.14
  204.6 3.2 collective-permute-start.15
  212.1 3.4 collective-permute-start.16
  214.1 3.1 collective-permute-start.17
  218.2 3.6 %collective-permute-start.18 = (f32[1,3,4,1024]{3,2,1,0:T(4,128)S(1)}, f32[1,3,4,1024]{3,2,1,0:T(4,128)S(1)}, u32[]{:S(2)}, u32[]{:S(2)}) collective-permute-start(f32[1,3,4,1024]{3,2,1,0:T(4,128)S(1)} %get-tuple-element.186), channel_id=1, source_target_pairs={{0,1},{2,3},{4,5},{6,7},{8,9},{10,11},{12,13},{14,15},{16,17},{18,... | collective-permute-start | bytes 147464 | tf_op jit(solution)/shard_map/ppermute | solution.py:21
  220.3 3.1 collective-permute-start.19
  227.0 3.4 collective-permute-start.20
  229.1 3.2 collective-permute-start.21
  235.6 97.3 %copy-start = (f32[3,2,1024]{2,1,0:T(2,128)S(1)}, f32[3,2,1024]{2,1,0:T(2,128)}, u32[]{:S(2)}) copy-start(f32[3,2,1024]{2,1,0:T(2,128)} %param.5) | copy-start | bytes 73732
Sparse Core Ops, SparseCore 0:
  101.5 89.3 all-gather.2
  237.2 92.2 all-gather.4
